TPU v7x, 32 devices: a whole 2x2x4 slice. The times are simulated.
32 devices in a mesh: prow: 4 (over y, x), pcol: 8 (over z, core).
Axes of the slice: x: 2, y: 2, z: 4, core: 2. Of those that a mesh axis runs over, the one named last changes fastest.
Arguments:
- schur: float32 [4, 4, 128, 2, 8, 128], P(None, 'prow', None, None, 'pcol'), may hold values from -0.125 to 0.125
- panel_inverse: float32 [2, 8, 128, 2, 4, 128], P(None, 'pcol', None, None, 'prow'), may hold values from -0.1875 to 0.1875
- coupling: float32 [4, 4, 128, 256], P(None, 'prow'), may hold values from -6 to 6
- zslab: float32 [4, 4, 128, 2, 8, 128], P(None, 'prow', None, None, 'pcol')
- targets: int32 [128], replicated, may hold values from 0 to 254
- pair_flags: int32 [128], replicated, may hold values 0 or 1
Outputs:
- eigenvectors: float32 [4, 4, 128, 128], P(None, 'prow', 'pcol')
All inputs are finite; a program needn't handle non-finite values.
Results may differ from a plain program's by a relative error of at most 0.0001.
Values sent between devices are 32-bit elements; how exact they have to be, the bound alone decides.
A program may use at most 64 MiB of HBM per device.

v0:
```python
import jax
import jax.numpy as jnp
from jax import lax
from jax.sharding import PartitionSpec as P

EPSILON = 1e-06


def shards(schur, panel_inverse, coupling, zslab, targets, pair_flags):
    block_size = schur.shape[2]
    row_blocks = schur.shape[0]
    col_blocks = schur.shape[3]
    ratio_rows = panel_inverse.shape[3]
    window = coupling.shape[3]
    vector_count = targets.shape[0]
    zrow_blocks = zslab.shape[0]
    panel_rows = ratio_rows * block_size
    triangle = schur.reshape(row_blocks * block_size, col_blocks * block_size)
    inverse = panel_inverse.reshape(col_blocks, block_size, panel_rows)
    strip_rows = coupling.reshape(row_blocks * block_size, window)
    z_rows = zslab.reshape(zrow_blocks * block_size, col_blocks * block_size)
    columns = jnp.arange(window, dtype=jnp.int32)[:, None]
    selection = (columns == targets[None, :]).astype(jnp.float32) + pair_flags[None, :].astype(
        jnp.float32
    ) * (columns == targets[None, :] + 1).astype(jnp.float32)
    right_side = -jnp.dot(strip_rows, selection, precision=lax.Precision.HIGHEST)
    pieces = [None] * col_blocks
    for panel_index in reversed(range(col_blocks)):
        residual = right_side[panel_index * panel_rows : (panel_index + 1) * panel_rows]
        if panel_index < col_blocks - 1:
            later_rows = jnp.concatenate(pieces[panel_index + 1 :], axis=0)
            partial_value = jnp.dot(
                triangle[
                    panel_index * panel_rows : (panel_index + 1) * panel_rows,
                    (panel_index + 1) * block_size :,
                ],
                later_rows,
                precision=lax.Precision.HIGHEST,
            )
            residual = residual - lax.psum(partial_value, "pcol")
        applied = jnp.dot(inverse[panel_index], residual, precision=lax.Precision.HIGHEST)
        pieces[panel_index] = lax.psum(applied, "prow")
    transformed = jnp.dot(z_rows, jnp.concatenate(pieces, axis=0), precision=lax.Precision.HIGHEST)
    stacked = transformed.reshape(zrow_blocks, 1, block_size, vector_count)
    total_rows = zrow_blocks * block_size * lax.axis_size("prow")
    summed = lax.psum(stacked, "pcol")
    squares = lax.psum(jnp.sum(summed * summed, axis=(0, 1, 2)), "prow")
    share_rows = block_size // lax.axis_size("pcol")
    owned_rows = lax.dynamic_slice_in_dim(
        summed, lax.axis_index("pcol") * share_rows, share_rows, 2
    )
    divisor = jnp.sqrt(squares / total_rows + EPSILON)
    return owned_rows / divisor[None, None, None, :]


def solution(mesh):
    in_specs = (
        P(None, "prow", None, None, "pcol", None),
        P(None, "pcol", None, None, "prow", None),
        P(None, "prow", None, None),
        P(None, "prow", None, None, "pcol", None),
        P(),
        P(),
    )
    out_specs = P(None, "prow", "pcol", None)
    return jax.shard_map(shards, mesh=mesh, in_specs=in_specs, out_specs=out_specs, check_vma=False)
```

profile of v0, /device:TPU:0, one launch (start us, length us, event | category | flops | bytes accessed | tf_op | source)
XLA Modules:
  0.0 233.2 jit_solution(16619724533023797762)
XLA Ops:
  6.5 1.8 slice_reduce_fusion
  8.4 0.0 copy-start.4
  8.4 0.6 copy-done.4
  9.1 0.7 fusion
  9.8 0.9 convolution_bitcast_fusion.3
  10.7 0.0 all-reduce.5.cloned.1.call-update
  10.7 0.0 all-reduce.7.cloned.1.call-start
  10.8 0.0 copy-start.1
  10.8 44.6 %all-reduce.5.cloned.1.call-done = f32[128,128]{0,1:T(8,128)} async-done(((f32[128,128]{0,1:T(8,128)}), f32[128,128]{0,1:T(8,128)}) %all-reduce.5.cloned.1.call-update) | async-done | bytes 65552 | tf_op jit(solution)/shard_map/psum | solution.py:42
  55.4 1.8 convolution_bitcast_fusion.1
  57.2 0.0 all-reduce.7.cloned.1.call-update
  57.2 0.0 all-reduce.9.cloned.1.call-start
  57.3 55.4 %all-reduce.7.cloned.1.call-done = f32[256,128]{0,1:T(8,128)} async-done(((f32[256,128]{0,1:T(8,128)}), f32[256,128]{0,1:T(8,128)}) %all-reduce.7.cloned.1.call-update) | async-done | bytes 131088 | tf_op jit(solution)/shard_map/psum | solution.py:40
  112.7 1.8 convolution_bitcast_fusion.2
  114.5 0.0 all-reduce.9.cloned.1.call-update
  114.5 0.0 all-reduce.11.cloned.1.call-start
  114.5 41.9 %all-reduce.9.cloned.1.call-done = f32[128,128]{0,1:T(8,128)} async-done(((f32[128,128]{0,1:T(8,128)}), f32[128,128]{0,1:T(8,128)}) %all-reduce.9.cloned.1.call-update) | async-done | bytes 65552 | tf_op jit(solution)/shard_map/psum | solution.py:42
  156.5 1.5 convolution_bitcast_fusion
  158.0 0.8 copy.8
  158.8 0.0 all-reduce.11.cloned.1.call-update
  158.8 55.6 %all-reduce.11.cloned.1.call-done = f32[4,1,128,128]{3,2,1,0:T(8,128)} async-done(((f32[4,1,128,128]{3,2,1,0:T(8,128)}), f32[4,1,128,128]{3,2,1,0:T(8,128)}) %all-reduce.11.cloned.1.call-update) | async-done | bytes 262160 | tf_op jit(solution)/shard_map/psum | solution.py:46
  214.4 1.0 multiply_reduce_fusion
  215.4 9.8 %psum.39 = f32[128]{0:T(128)S(1)} all-reduce(f32[128]{0:T(128)S(1)} %multiply_reduce_fusion), channel_id=1, replica_groups=mesh['prow'=4,'pcol'=8] {'prow'}, use_global_device_ids=true, to_apply=%region_5.0 | all-reduce | flops 128 | bytes 1024 | tf_op jit(solution)/shard_map/psum | solution.py:47
  225.3 1.4 dynamic-slice_divide_fusion
  (14 shorter events, 0.1 us)
Async XLA Ops:
  6.5 2.5 %copy-start = (f32[4,1,128,256]{3,2,1,0:T(8,128)S(1)}, f32[4,1,128,256]{3,2,1,0:T(8,128)}, u32[]{:S(2)}) copy-start(f32[4,1,128,256]{3,2,1,0:T(8,128)} %param.8) | copy-start | bytes 1572868
  6.5 1.8 copy-start.5
  6.5 48.9 %all-reduce.5.cloned.1.call-start = ((), (), s32[]{:S(2)}) async-start(), calls=%async_computation | async-start | bytes 131072 | tf_op jit(solution)/shard_map/psum | solution.py:42
  8.4 0.7 copy-start.4
  9.1 1.7 copy-start.2
  10.7 102.0 %all-reduce.7.cloned.1.call-start = ((), (), s32[]{:S(2)}) async-start(), calls=%async_computation.1 | async-start | bytes 262144 | tf_op jit(solution)/shard_map/psum | solution.py:40
  10.8 145.7 %copy-start.1 = (f32[4,1,128,2,1,128]{5,4,3,2,1,0:T(1,128)S(1)}, f32[4,1,128,2,1,128]{5,4,3,2,1,0:T(1,128)}, u32[]{:S(2)}) copy-start(f32[4,1,128,2,1,128]{5,4,3,2,1,0:T(1,128)} %param.9) | copy-start | bytes 1572868
  57.2 99.3 %all-reduce.9.cloned.1.call-start = ((), (), s32[]{:S(2)}) async-start(), calls=%async_computation.2 | async-start | bytes 131072 | tf_op jit(solution)/shard_map/psum | solution.py:42
  114.5 42.0 %copy-start.3 = (f32[128,128]{0,1:T(8,128)S(1)}, f32[128,128]{0,1:T(8,128)}, u32[]{:S(2)}) copy-start(f32[128,128]{0,1:T(8,128)} %all-reduce.5.cloned.1.call-done) | copy-start | bytes 196612
  114.5 99.9 %all-reduce.11.cloned.1.call-start = ((), (), s32[]{:S(2)}) async-start(), calls=%async_computation.3 | async-start | bytes 524288 | tf_op jit(solution)/shard_map/psum | solution.py:46
Sparse Core Ops, SparseCore 0:
  10.8 44.5 all-reduce.4
  57.7 54.9 all-reduce.6
  115.5 40.8 all-reduce.8
  158.9 55.4 all-reduce.10
where the time goes:
time: 234 us; the launch traced here: 233 us
  waiting for transfers between devices  198 us (85%)
  between operations  13.2 us (6%)
  blocking collectives  9.84 us (4%)
  matrix products  6.66 us (3%)
  local copies, waits for them, and re-layouts  3.37 us (1%)
  other arithmetic  2.44 us (1%)
    psum x2, waiting for transfers between devices, shards(): pieces[panel_index] = lax.psum(applied, 'prow')  86.5 us
    psum x1, waiting for transfers between devices, shards(): summed = lax.psum(stacked, 'pcol')  55.6 us
    psum x1, waiting for transfers between devices, shards(): residual = residual - lax.psum(partial_value, 'pcol')  55.4 us
    psum x1, blocking collectives, shards(): squares = lax.psum(jnp.sum(summed * summed, axis=(0, 1, 2)), 'prow')  9.84 us
  transfers between devices with their start and end apart: 4, of which 4 were waited for; matrix products, arithmetic and copies ran while one was open for 0% of the time, Pallas kernels for 0%

commit v1 on v0

--- a/solution.py
+++ b/solution.py
@@ -2,6 +2,7 @@
 import jax.numpy as jnp
 from jax import lax
 from jax.sharding import PartitionSpec as P
+from jax.lax import all_gather
 
 EPSILON = 1e-06
 
@@ -37,7 +38,7 @@
                 later_rows,
                 precision=lax.Precision.HIGHEST,
             )
-            residual = residual - lax.psum(partial_value, "pcol")
+            residual = residual - jnp.sum(all_gather(partial_value, axis_name="pcol"), axis=0)
         applied = jnp.dot(inverse[panel_index], residual, precision=lax.Precision.HIGHEST)
         pieces[panel_index] = lax.psum(applied, "prow")
     transformed = jnp.dot(z_rows, jnp.concatenate(pieces, axis=0), precision=lax.Precision.HIGHEST)

time: 234 us -> 201 us (0.86)
  waiting for transfers between devices: 198 us -> 164 us
    psum x1 -> x0, waiting for transfers between devices: 55.4 us -> none  [shards(): residual = residual - lax.psum(partial_value, 'pcol')]
    all_gather x0 -> x1, waiting for transfers between devices: none -> 22.4 us  [shards(): all_gather(partial_value, axis_name='pcol')]
where the time goes in v1:
time: 201 us
  waiting for transfers between devices  164 us (82%)
  between operations  13.2 us (7%)
  blocking collectives  9.84 us (5%)
  matrix products  5.75 us (3%)
  local copies, waits for them, and re-layouts  4.93 us (2%)
  other arithmetic  2.69 us (1%)
    psum x2, waiting for transfers between devices, shards(): pieces[panel_index] = lax.psum(applied, 'prow')  86.1 us
    psum x1, waiting for transfers between devices, shards(): summed = lax.psum(stacked, 'pcol')  55.6 us
    all_gather x1, waiting for transfers between devices, shards(): all_gather(partial_value, axis_name='pcol')  22.4 us
    psum x1, blocking collectives, shards(): squares = lax.psum(jnp.sum(summed * summed, axis=(0, 1, 2)), 'prow')  9.84 us
  transfers between devices with their start and end apart: 4, of which 4 were waited for; matrix products, arithmetic and copies ran while one was open for 0% of the time, Pallas kernels for 0%

profile of v1, /device:TPU:0, one launch (start us, length us, event | category | flops | bytes accessed | tf_op | source)
XLA Modules:
  0.0 200.7 jit_solution(12079543562359833911)
XLA Ops:
  6.5 1.8 slice_reduce_fusion
  8.4 0.6 copy-done.4
  9.1 0.7 fusion
  9.8 0.9 convolution_bitcast_fusion.3
  10.7 0.0 all-reduce.4.cloned.1.call-update
  10.7 0.0 all-gather.3.cloned.1.call-start
  10.8 44.6 %all-reduce.4.cloned.1.call-done = f32[128,128]{0,1:T(8,128)} async-done(((f32[128,128]{0,1:T(8,128)}), f32[128,128]{0,1:T(8,128)}) %all-reduce.4.cloned.1.call-update) | async-done | bytes 65552 | tf_op jit(solution)/shard_map/psum | solution.py:43
  55.4 1.8 convolution_bitcast_fusion.1
  57.2 0.0 all-gather.3.cloned.1.call-update
  57.2 0.0 all-reduce.6.cloned.1.call-start
  57.2 22.4 %all-gather.3.cloned.1.call-done = f32[2048,128]{0,1:T(8,128)} async-done(((f32[256,128]{0,1:T(8,128)}), f32[2048,128]{0,1:T(8,128)}) %all-gather.3.cloned.1.call-update) | async-done | bytes 1048592 | tf_op jit(solution)/shard_map/all_gather | solution.py:41
  79.6 1.6 copy.11
  81.2 0.3 bitcast_reduce_fusion
  81.5 0.9 convolution_bitcast_fusion.2
  82.3 0.0 all-reduce.6.cloned.1.call-update
  82.4 0.0 all-reduce.8.cloned.1.call-start
  82.4 41.5 %all-reduce.6.cloned.1.call-done = f32[128,128]{0,1:T(8,128)} async-done(((f32[128,128]{0,1:T(8,128)}), f32[128,128]{0,1:T(8,128)}) %all-reduce.6.cloned.1.call-update) | async-done | bytes 65552 | tf_op jit(solution)/shard_map/psum | solution.py:43
  124.0 1.5 convolution_bitcast_fusion
  125.5 0.8 copy.8
  126.3 0.0 all-reduce.8.cloned.1.call-update
  126.3 55.6 %all-reduce.8.cloned.1.call-done = f32[4,1,128,128]{3,2,1,0:T(8,128)} async-done(((f32[4,1,128,128]{3,2,1,0:T(8,128)}), f32[4,1,128,128]{3,2,1,0:T(8,128)}) %all-reduce.8.cloned.1.call-update) | async-done | bytes 262160 | tf_op jit(solution)/shard_map/psum | solution.py:47
  181.9 1.0 multiply_reduce_fusion
  182.9 9.8 %psum.31 = f32[128]{0:T(128)S(1)} all-reduce(f32[128]{0:T(128)S(1)} %multiply_reduce_fusion), channel_id=1, replica_groups=mesh['prow'=4,'pcol'=8] {'prow'}, use_global_device_ids=true, to_apply=%region_5.0 | all-reduce | flops 128 | bytes 1024 | tf_op jit(solution)/shard_map/psum | solution.py:48
  192.8 1.4 dynamic-slice_divide_fusion
  (16 shorter events, 0.1 us)
Async XLA Ops:
  6.5 2.5 %copy-start = (f32[4,1,128,256]{3,2,1,0:T(8,128)S(1)}, f32[4,1,128,256]{3,2,1,0:T(8,128)}, u32[]{:S(2)}) copy-start(f32[4,1,128,256]{3,2,1,0:T(8,128)} %param.8) | copy-start | bytes 1572868
  6.5 1.8 copy-start.5
  6.5 48.9 %all-reduce.4.cloned.1.call-start = ((), (), s32[]{:S(2)}) async-start(), calls=%async_computation | async-start | bytes 131072 | tf_op jit(solution)/shard_map/psum | solution.py:43
  8.4 0.7 copy-start.4
  9.1 1.7 copy-start.2
  10.7 68.9 %all-gather.3.cloned.1.call-start = ((), (), s32[]{:S(2)}) async-start(), calls=%async_computation.3 | async-start | bytes 1179648 | tf_op jit(solution)/shard_map/all_gather | solution.py:41
  57.2 66.8 %all-reduce.6.cloned.1.call-start = ((), (), s32[]{:S(2)}) async-start(), calls=%async_computation.1 | async-start | bytes 131072 | tf_op jit(solution)/shard_map/psum | solution.py:43
  81.2 42.8 %copy-start.3 = (f32[128,128]{0,1:T(8,128)S(1)}, f32[128,128]{0,1:T(8,128)}, u32[]{:S(2)}) copy-start(f32[128,128]{0,1:T(8,128)} %all-reduce.4.cloned.1.call-done) | copy-start | bytes 196612
  81.4 42.5 %copy-start.1 = (f32[4,1,128,2,1,128]{5,4,3,2,1,0:T(1,128)S(1)}, f32[4,1,128,2,1,128]{5,4,3,2,1,0:T(1,128)}, u32[]{:S(2)}) copy-start(f32[4,1,128,2,1,128]{5,4,3,2,1,0:T(1,128)} %param.9) | copy-start | bytes 1572868
  82.4 99.5 %all-reduce.8.cloned.1.call-start = ((), (), s32[]{:S(2)}) async-start(), calls=%async_computation.2 | async-start | bytes 524288 | tf_op jit(solution)/shard_map/psum | solution.py:47
Sparse Core Ops, SparseCore 0:
  10.8 44.5 all-reduce.3
  57.3 22.2 all-gather.2
  82.5 41.4 all-reduce.5
  126.4 55.4 all-reduce.7
